TPU v7x, 256 devices: a whole 4x4x8 slice. The times are simulated.
256 devices in a mesh: section: 2 (over z_hi), gy: 32 (over z_lo, x, core), gz: 4 (over y).
Axes of the slice: x: 4, y: 4, z: 8 (z_hi: 2, z_lo: 4; z = z_hi * 4 + z_lo), core: 2. Of those that a mesh axis runs over, the one named last changes fastest.
Arguments:
- inflow: float32 [2, 64, 2, 64, 512], P(None, None, None, 'gy', 'gz'), may hold values from -6 to 6
- weights: float32 [4, 27, 64, 64], P('section'), may hold values from -0.15625 to 0.15625
- biases: float32 [4, 64], P('section'), may hold values from -3 to 3
- cotangent: float32 [2, 64, 2, 64, 512], P(None, None, None, 'gy', 'gz'), may hold values from -6 to 6
Outputs:
- section_out: float32 [2, 2, 64, 2, 64, 512], P('section', None, None, None, 'gy', 'gz')
- section_grad: float32 [2, 2, 64, 2, 64, 512], P('section', None, None, None, 'gy', 'gz')
- weight_grad: float32 [4, 27, 64, 64], P('section')
- bias_grad: float32 [4, 64], P('section')
All inputs are finite; a program needn't handle non-finite values.
Results may differ from a plain program's by a relative error of at most 0.0001.
Values sent between devices are 32-bit elements; how exact they have to be, the bound alone decides.
A program may use at most 128 MiB of HBM per device.

v0:
```python
import math
import jax
import jax.numpy as jnp
from jax import lax
from jax.sharding import PartitionSpec as P


def extended(block, sides, width):
    for axis, dim in sides:
        count = lax.axis_size(axis)
        forward = [(i, i + 1) for i in range(count - 1)]
        backward = [(target, source) for source, target in forward]
        low = lax.ppermute(
            lax.slice_in_dim(block, block.shape[dim] - width, None, axis=dim), axis, forward
        )
        high = lax.ppermute(lax.slice_in_dim(block, 0, width, axis=dim), axis, backward)
        block = jnp.concatenate([low, block, high], axis=dim)
    return block


def passed_along(block, axis, distance):
    devices = range(lax.axis_size(axis))
    route = [(i - distance, i) for i in devices if i - distance in devices]
    return lax.ppermute(block, axis, route)


def stacked_taps(padded, out_sizes, flipped):
    size_x, size_y, size_z = out_sizes
    pieces = []
    for offset in range(27):
        start_x, start_y, start_z = (offset // 9, offset // 3 % 3, offset % 3)
        if flipped:
            start_x, start_y, start_z = (2 - start_x, 2 - start_y, 2 - start_z)
        pieces.append(
            padded[
                :,
                start_x : start_x + size_x,
                start_y : start_y + size_y,
                start_z : start_z + size_z,
            ]
        )
    return jnp.stack(pieces)


def convolve(weight, padded, out_sizes):
    return jnp.einsum(
        "toc,tcxyz->oxyz",
        weight,
        stacked_taps(padded, out_sizes, False),
        precision=lax.Precision.HIGHEST,
    )


def face_rim(values):
    rimmed = extended(values, (("gy", 2), ("gz", 3)), 1)
    return jnp.pad(rimmed, ((0, 0), (1, 1), (0, 0), (0, 0)))


def slope_rim(values):
    rimmed = extended(values, (("gy", 2), ("gz", 3)), 1)
    return jnp.pad(rimmed, ((0, 0), (1, 1), (0, 0), (0, 0)))


def section_forward(weights, biases, current, extents):
    stored = []
    for layer_index in range(weights.shape[0]):
        padded = face_rim(current)
        pre_act = (
            convolve(weights[layer_index], padded, extents)
            + biases[layer_index][:, None, None, None]
        )
        stored.append((padded, pre_act))
        current = jax.nn.silu(pre_act)
    return (stored, current)


def per_device(inflow, weights, biases, cotangent):
    highest = lax.Precision.HIGHEST
    first_section = lax.axis_index("section") == 0
    micro_count = inflow.shape[0]
    layer_count = weights.shape[0]
    extents = inflow.shape[2:]
    blank = jnp.zeros(inflow.shape[1:], jnp.float32)
    received = blank
    stored_all = []
    produced = []
    for step_index in range(micro_count + 1):
        own_input = inflow[step_index] if step_index < micro_count else blank
        current = jnp.where(first_section, own_input, received)
        stored, current = section_forward(weights, biases, current, extents)
        stored_all.append(stored)
        produced.append(current)
        if step_index < micro_count:
            received = passed_along(current, "section", 1)
    section_out = jnp.stack(
        [
            jnp.where(first_section, produced[micro], produced[micro + 1])
            for micro in range(micro_count)
        ]
    )
    cell_count = (
        micro_count
        * extents[0]
        * extents[1]
        * lax.axis_size("gy")
        * extents[2]
        * lax.axis_size("gz")
    )
    grad_scale = 1.0 / math.sqrt(cell_count)
    weight_grads = [jnp.zeros(weights.shape[1:], jnp.float32) for layer_index in range(layer_count)]
    bias_grads = [jnp.zeros(biases.shape[1:], jnp.float32) for layer_index in range(layer_count)]
    returned = blank
    collected = []
    for step_index in range(micro_count + 1):
        later = micro_count - 1 - step_index
        own_grad = cotangent[later] if later >= 0 else blank
        gradient = jnp.where(first_section, returned, own_grad)
        stored = stored_all[micro_count - step_index]
        for layer_index in reversed(range(layer_count)):
            padded, pre_act = stored[layer_index]
            sigmoid_value = jax.nn.sigmoid(pre_act)
            slope_grad = gradient * sigmoid_value * (1.0 + pre_act * (1.0 - sigmoid_value))
            weight_grads[layer_index] = weight_grads[layer_index] + jnp.einsum(
                "oxyz,tcxyz->toc",
                slope_grad,
                stacked_taps(padded, extents, False),
                precision=highest,
            )
            bias_grads[layer_index] = bias_grads[layer_index] + jnp.sum(slope_grad, axis=(1, 2, 3))
            gradient = jnp.einsum(
                "toc,toxyz->cxyz",
                weights[layer_index],
                stacked_taps(slope_rim(slope_grad), extents, True),
                precision=highest,
            )
        collected.append(gradient)
        if step_index < micro_count:
            returned = passed_along(gradient, "section", -1)
    section_grad = jnp.stack(
        [
            jnp.where(
                first_section, collected[micro_count - micro], collected[micro_count - 1 - micro]
            )
            for micro in range(micro_count)
        ]
    )
    weight_total, bias_total = lax.psum(
        (jnp.stack(weight_grads) * grad_scale, jnp.stack(bias_grads) * grad_scale), ("gy", "gz")
    )
    return (section_out[None], section_grad[None], weight_total, bias_total)


def solution(mesh):
    return jax.shard_map(
        per_device,
        mesh=mesh,
        in_specs=(
            P(None, None, None, "gy", "gz"),
            P("section", None, None, None),
            P("section", None),
            P(None, None, None, "gy", "gz"),
        ),
        out_specs=(
            P("section", None, None, None, "gy", "gz"),
            P("section", None, None, None, "gy", "gz"),
            P("section", None, None, None),
            P("section", None),
        ),
        check_vma=False,
    )
```

profile of v0, /device:TPU:8, one launch (start us, length us, event | category | flops | bytes accessed | tf_op | source)
XLA Modules:
  0.0 1630.1 jit_solution(7726312461387545481)
XLA Ops:
  11.3 3.1 collective-permute-done.1
  14.6 3.5 collective-permute-start.2
  23.6 3.8 collective-permute-done.3
  32.4 3.5 collective-permute-start.4
  37.2 4.1 collective-permute-done.5
  41.4 3.2 collective-permute-start.6
  47.3 3.2 collective-permute-done.6
  50.5 3.5 collective-permute-done.7
  59.0 9.1 collective-permute-start.8
  68.1 3.3 collective-permute-done.8
  75.4 4.7 collective-permute-done.10
  82.2 4.2 collective-permute-start.12
  96.2 3.8 collective-permute-start.13
  101.3 4.0 collective-permute-done.14
  107.7 3.7 collective-permute-start.16
  111.3 3.2 collective-permute-done.15
  122.1 8.2 collective-permute-start.17
  130.3 3.2 collective-permute-done.17
  137.6 3.2 collective-permute-done.19
  143.2 3.7 collective-permute-start.21
  146.8 3.2 collective-permute-done.20
  157.5 3.5 collective-permute-start.22
  162.3 4.1 collective-permute-done.23
  168.5 4.4 collective-permute-start.25
  182.8 3.8 collective-permute-start.26
  187.9 3.3 collective-permute-done.27
  193.3 3.9 collective-permute-start.29
  197.2 3.2 collective-permute-done.28
  207.2 3.8 collective-permute-start.30
  212.2 3.8 collective-permute-done.31
  218.2 3.9 collective-permute-start.33
  222.1 3.2 collective-permute-done.32
  233.2 10.2 collective-permute-done.34
  247.7 4.6 collective-permute-done.36
  254.8 3.6 collective-permute-start.38
  269.0 3.5 collective-permute-start.39
  278.4 3.7 collective-permute-start.42
  293.9 3.0 fusion.24
  296.9 7.1 collective-permute-done.43
  304.2 3.0 convolution_bitcast_fusion
  310.8 3.0 fusion.27
  316.8 4.2 collective-permute-start.47
  330.6 3.0 fusion.23
  335.1 3.8 collective-permute-start.48
  340.2 3.6 collective-permute-done.49
  345.9 3.9 collective-permute-start.51
  349.8 333.4 %psum.15 = f32[2,64]{1,0:T(2,128)} all-reduce(f32[2,64]{1,0:T(2,128)S(1)} %maximum_multiply_fusion.1), channel_id=1, replica_groups=mesh['section'=2,'gy'=32,'gz'=4] {'gy','gz'}, use_global_device_ids=true, to_apply=%region_7.8 | all-reduce | flops 128 | bytes 1024 | tf_op jit(solution)/shard_map/psum | solution.py:147
  688.9 931.3 %all-reduce.14.cloned.1.call-done = f32[2,27,64,64]{2,3,1,0:T(8,128)} async-done(((f32[2,27,64,64]{2,3,1,0:T(8,128)}), f32[2,27,64,64]{2,3,1,0:T(8,128)}) %all-reduce.14.cloned.1.call-update) | async-done | bytes 884752 | tf_op jit(solution)/shard_map/psum | solution.py:147
  (482 shorter events, 161.3 us)
Async XLA Ops:
  7.2 1613.0 %all-reduce.14.cloned.1.call-start = ((), (), s32[]{:S(2)}) async-start(), calls=%async_computation | async-start | bytes 3538944 | tf_op jit(solution)/shard_map/psum | solution.py:147
  10.0 4.4 collective-permute-start.1
  14.6 9.0 collective-permute-start.2
  18.1 9.3 collective-permute-start.3
  32.4 4.8 collective-permute-start.4
  35.9 5.4 collective-permute-start.5
  41.4 9.0 collective-permute-start.6
  44.6 9.3 collective-permute-start.7
  59.0 12.4 collective-permute-start.8
  74.0 6.0 collective-permute-start.10
  80.2 9.0 collective-permute-start.11
  82.2 9.0 collective-permute-start.12
  96.2 5.1 collective-permute-start.13
  100.0 5.3 collective-permute-start.14
  105.5 9.0 collective-permute-start.15
  107.7 9.3 collective-permute-start.16
  122.1 11.4 collective-permute-start.17
  136.3 4.5 collective-permute-start.19
  141.0 9.0 collective-permute-start.20
  143.2 9.3 collective-permute-start.21
  157.5 4.8 collective-permute-start.22
  161.0 5.4 collective-permute-start.23
  166.6 9.0 collective-permute-start.24
  168.5 9.0 collective-permute-start.25
  182.8 5.1 collective-permute-start.26
  186.6 4.6 collective-permute-start.27
  191.3 9.0 collective-permute-start.28
  193.3 9.0 collective-permute-start.29
  207.2 5.1 collective-permute-start.30
  210.9 5.1 collective-permute-start.31
  216.2 9.0 collective-permute-start.32
  218.2 9.1 collective-permute-start.33
  231.9 11.5 collective-permute-start.34
  246.4 5.9 collective-permute-start.36
  252.4 9.0 collective-permute-start.37
  254.8 9.3 collective-permute-start.38
  269.0 5.7 collective-permute-start.39
  276.3 9.0 collective-permute-start.41
  278.4 9.3 collective-permute-start.42
  292.4 11.6 collective-permute-start.43
  307.2 6.6 collective-permute-start.44
  309.5 5.1 collective-permute-start.45
  314.8 9.0 collective-permute-start.46
  316.8 9.0 collective-permute-start.47
  335.1 5.1 collective-permute-start.48
  338.9 4.9 collective-permute-start.49
  344.0 339.3 %collective-permute-start.50 = (f32[64,2,4,1]{3,0,2,1:T(8,128)S(1)}, f32[64,2,4,1]{3,0,2,1:T(8,128)S(1)}, u32[]{:S(2)}, u32[]{:S(2)}) collective-permute-start(f32[64,2,4,1]{3,0,2,1:T(8,128)S(1)} %get-tuple-element.22), channel_id=1, source_target_pairs={{0,1},{1,2},{2,3},{4,5},{5,6},{6,7},{8,9},{9,10},{10,11},{12,13},{... | collective-permute-start | bytes 6152 | tf_op jit(solution)/shard_map/ppermute | solution.py:13
  345.9 337.4 %collective-permute-start.51 = (f32[64,2,4,1]{3,0,2,1:T(8,128)S(1)}, f32[64,2,4,1]{3,0,2,1:T(8,128)S(1)}, u32[]{:S(2)}, u32[]{:S(2)}) collective-permute-start(f32[64,2,4,1]{3,0,2,1:T(8,128)S(1)} %get-tuple-element.23), channel_id=1, source_target_pairs={{1,0},{2,1},{3,2},{5,4},{6,5},{7,6},{9,8},{10,9},{11,10},{13,12},{... | collective-permute-start | bytes 6152 | tf_op jit(solution)/shard_map/ppermute | solution.py:16
  (7 other events, 38.3 us)
Sparse Core Ops, SparseCore 0:
  335.3 1284.8 all-reduce.13
where the time goes:
time: 1640 us; the launch traced here: 1630 us
  waiting for transfers between devices  1050 us (64%)
  blocking collectives  333 us (20%)
  starting transfers between devices  144 us (9%)
  matrix products  46.1 us (3%)
  local copies, waits for them, and re-layouts  22.3 us (1%)
  between operations  18 us (1%)
    psum x1, waiting for transfers between devices, per_device(): lax.psum((jnp.stack(weight_grads) * grad_scale, jnp.stack(bias_grads) * g...  931 us
    psum x1, blocking collectives, per_device(): lax.psum((jnp.stack(weight_grads) * grad_scale, jnp.stack(bias_grads) * g...  333 us
    ppermute x24, waiting for transfers between devices, extended(): lax.ppermute(lax.slice_in_dim(block, 0, width, axis=dim), axis, backward)  67.7 us
    ppermute x24, starting transfers between devices, extended(): lax.ppermute(lax.slice_in_dim(block, block.shape[dim] - width, None, axis...  64.7 us
    ppermute x24, starting transfers between devices, extended(): lax.ppermute(lax.slice_in_dim(block, 0, width, axis=dim), axis, backward)  59.7 us
  transfers between devices with their start and end apart: 53, of which 38 were waited for; matrix products, arithmetic and copies ran while one was open for 1% of the time, Pallas kernels for 0%

commit v1 on v0

--- a/solution.py
+++ b/solution.py
@@ -145,7 +145,8 @@
         ]
     )
     weight_total, bias_total = lax.psum(
-        (jnp.stack(weight_grads) * grad_scale, jnp.stack(bias_grads) * grad_scale), ("gy", "gz")
+        lax.psum((jnp.stack(weight_grads) * grad_scale, jnp.stack(bias_grads) * grad_scale), "gz"),
+        "gy",
     )
     return (section_out[None], section_grad[None], weight_total, bias_total)
 

time: 1640 us -> 749 us (0.46)
  waiting for transfers between devices: 1050 us -> 386 us
  blocking collectives: 333 us -> 85.2 us
    psum x1, waiting for transfers between devices: 931 us -> 0.01 us  [per_device(): lax.psum((jnp.stack(weight_grads) * grad_scale, jnp.stack(bias_grads) * g...]
    psum x1, blocking collectives: 333 us -> 15.9 us  [per_device(): lax.psum((jnp.stack(weight_grads) * grad_scale, jnp.stack(bias_grads) * g...]
    psum x0 -> x1, waiting for transfers between devices: none -> 267 us  [per_device(): lax.psum(lax.psum((jnp.stack(weight_grads) * grad_scale, jnp.stack(bias_g...]
    psum x0 -> x1, blocking collectives: none -> 69.3 us  [per_device(): lax.psum(lax.psum((jnp.stack(weight_grads) * grad_scale, jnp.stack(bias_g...]
  transfers between devices with their start and end apart: 53 -> 54, of which waited for: 38 -> 38; matrix products, arithmetic and copies ran while one was open for 1% -> 6% of each run, Pallas kernels for 0% -> 0%
where the time goes in v1:
time: 749 us; the launch traced here: 741 us
  waiting for transfers between devices  386 us (52%)
  starting transfers between devices  145 us (19%)
  blocking collectives  85.2 us (11%)
  matrix products  48.1 us (6%)
  local copies, waits for them, and re-layouts  34.8 us (5%)
  other arithmetic  24.8 us (3%)
  between operations  17.8 us (2%)
    psum x1, waiting for transfers between devices, per_device(): lax.psum(lax.psum((jnp.stack(weight_grads) * grad_scale, jnp.stack(bias_g...  267 us
    psum x1, blocking collectives, per_device(): lax.psum(lax.psum((jnp.stack(weight_grads) * grad_scale, jnp.stack(bias_g...  69.3 us
    ppermute x24, waiting for transfers between devices, extended(): lax.ppermute(lax.slice_in_dim(block, 0, width, axis=dim), axis, backward)  67.8 us
    ppermute x24, starting transfers between devices, extended(): lax.ppermute(lax.slice_in_dim(block, block.shape[dim] - width, None, axis...  64.7 us
    ppermute x24, starting transfers between devices, extended(): lax.ppermute(lax.slice_in_dim(block, 0, width, axis=dim), axis, backward)  59.7 us
    unnamed x222, local copies, waits for them, and re-layouts  30 us
    ppermute x24, waiting for transfers between devices, extended(): lax.ppermute(lax.slice_in_dim(block, block.shape[dim] - width, None, axis...  27 us
    ppermute x4, waiting for transfers between devices, passed_along(): return lax.ppermute(block, axis, route)  23.7 us
  transfers between devices with their start and end apart: 54, of which 38 were waited for; matrix products, arithmetic and copies ran while one was open for 6% of the time, Pallas kernels for 0%

profile of v1, /device:TPU:8, one launch (start us, length us, event | category | flops | bytes accessed | tf_op | source)
XLA Modules:
  0.0 741.2 jit_solution(17985590083612953827)
XLA Ops:
  11.3 3.1 collective-permute-done.1
  14.6 3.5 collective-permute-start.2
  23.6 3.8 collective-permute-done.3
  32.4 3.5 collective-permute-start.4
  37.2 4.1 collective-permute-done.5
  41.4 3.2 collective-permute-start.6
  47.3 3.2 collective-permute-done.6
  50.5 3.5 collective-permute-done.7
  59.0 9.1 %collective-permute-start.8 = (f32[64,2,2,128]{3,0,2,1:T(8,128)S(1)}, f32[64,2,2,128]{3,0,2,1:T(8,128)S(1)}, u32[]{:S(2)}, u32[]{:S(2)}) collective-permute-start(f32[64,2,2,128]{3,0,2,1:T(8,128)S(1)} %bitcast_multiply_fusion.12), channel_id=1, source_target_pairs={{0,128},{1,129},{2,130},{3,131},{4,132},{5,133},{6,134},{7,135},{8... | collective-permute-start | bytes 393224 | tf_op jit(solution)/shard_map/ppermute | solution.py:24
  68.1 3.3 collective-permute-done.8
  75.4 4.7 collective-permute-done.10
  82.2 4.2 collective-permute-start.12
  96.2 3.8 collective-permute-start.13
  101.3 4.0 collective-permute-done.14
  107.7 3.7 collective-permute-start.16
  111.3 3.2 collective-permute-done.15
  122.2 8.2 %collective-permute-start.17 = (f32[64,2,2,128]{3,0,2,1:T(8,128)S(1)}, f32[64,2,2,128]{3,0,2,1:T(8,128)S(1)}, u32[]{:S(2)}, u32[]{:S(2)}) collective-permute-start(f32[64,2,2,128]{3,0,2,1:T(8,128)S(1)} %get-tuple-element.21), channel_id=1, source_target_pairs={{0,128},{1,129},{2,130},{3,131},{4,132},{5,133},{6,134},{7,135},{8... | collective-permute-start | bytes 393224 | tf_op jit(solution)/shard_map/ppermute | solution.py:24
  130.3 3.2 collective-permute-done.17
  137.6 3.2 collective-permute-done.19
  143.2 3.7 collective-permute-start.21
  146.8 3.2 collective-permute-done.20
  157.6 3.5 collective-permute-start.22
  162.4 4.1 collective-permute-done.23
  168.5 4.4 collective-permute-start.25
  182.8 3.8 collective-permute-start.26
  187.9 3.3 collective-permute-done.27
  193.3 3.9 collective-permute-start.29
  197.2 3.2 collective-permute-done.28
  207.2 3.8 collective-permute-start.30
  212.3 3.8 collective-permute-done.31
  218.2 3.9 collective-permute-start.33
  222.1 3.2 collective-permute-done.32
  233.2 10.2 %collective-permute-done.34 = f32[64,2,2,128]{3,0,2,1:T(8,128)S(1)} collective-permute-done((f32[64,2,2,128]{3,0,2,1:T(8,128)S(1)}, f32[64,2,2,128]{3,0,2,1:T(8,128)S(1)}, u32[]{:S(2)}, u32[]{:S(2)}) %collective-permute-start.34) | collective-permute-done | bytes 131104 | tf_op jit(solution)/shard_map/ppermute | solution.py:24
  247.7 4.6 collective-permute-done.36
  254.8 3.6 collective-permute-start.38
  269.0 3.5 collective-permute-start.39
  278.4 3.7 collective-permute-start.42
  293.8 3.0 fusion.24
  296.9 7.0 collective-permute-done.43
  316.8 4.2 collective-permute-start.47
  330.6 3.0 fusion.23
  335.2 3.8 collective-permute-start.48
  340.3 3.6 collective-permute-done.49
  345.9 3.9 collective-permute-start.51
  349.9 15.9 %psum.30 = f32[2,64]{1,0:T(2,128)S(1)} all-reduce(f32[2,64]{1,0:T(2,128)S(1)} %maximum_multiply_fusion.1), channel_id=1, replica_groups=mesh['section'=2,'gy'=32,'gz'=4] {'gz'}, use_global_device_ids=true, to_apply=%region_8.9 | all-reduce | flops 128 | bytes 1024 | tf_op jit(solution)/shard_map/psum | solution.py:148
  365.8 69.3 %psum.31 = f32[2,64]{1,0:T(2,128)} all-reduce(f32[2,64]{1,0:T(2,128)S(1)} %psum.30), channel_id=1, replica_groups=mesh['section'=2,'gy'=32,'gz'=4] {'gy'}, use_global_device_ids=true, to_apply=%region_9.10 | all-reduce | flops 128 | bytes 1024 | tf_op jit(solution)/shard_map/psum | solution.py:147
  458.7 4.2 fusion
  463.9 267.3 %all-reduce.17.cloned.1.call-done = f32[2,27,64,64]{2,3,1,0:T(8,128)} async-done(((f32[2,27,64,64]{2,3,1,0:T(8,128)}), f32[2,27,64,64]{2,3,1,0:T(8,128)}) %all-reduce.17.cloned.1.call-update) | async-done | bytes 884752 | tf_op jit(solution)/shard_map/psum | solution.py:147
  (490 shorter events, 186.6 us)
Async XLA Ops:
  7.2 450.9 %all-reduce.15.cloned.1.call-start = ((), (), s32[]{:S(2)}) async-start(), calls=%async_computation | async-start | bytes 3538944 | tf_op jit(solution)/shard_map/psum | solution.py:148
  14.6 9.0 %collective-permute-start.2 = (f32[64,2,4,1]{3,0,2,1:T(8,128)S(1)}, f32[64,2,4,1]{3,0,2,1:T(8,128)S(1)}, u32[]{:S(2)}, u32[]{:S(2)}) collective-permute-start(f32[64,2,4,1]{3,0,2,1:T(8,128)S(1)} %get-tuple-element.48), channel_id=1, source_target_pairs={{0,1},{1,2},{2,3},{4,5},{5,6},{6,7},{8,9},{9,10},{10,11},{12,13},{... | collective-permute-start | bytes 6152 | tf_op jit(solution)/shard_map/ppermute | solution.py:13
  18.1 9.3 %collective-permute-start.3 = (f32[64,2,4,1]{3,0,2,1:T(8,128)S(1)}, f32[64,2,4,1]{3,0,2,1:T(8,128)S(1)}, u32[]{:S(2)}, u32[]{:S(2)}) collective-permute-start(f32[64,2,4,1]{3,0,2,1:T(8,128)S(1)} %get-tuple-element.49), channel_id=1, source_target_pairs={{1,0},{2,1},{3,2},{5,4},{6,5},{7,6},{9,8},{10,9},{11,10},{13,12},{... | collective-permute-start | bytes 6152 | tf_op jit(solution)/shard_map/ppermute | solution.py:16
  32.4 4.8 collective-permute-start.4
  35.9 5.4 collective-permute-start.5
  41.4 9.0 %collective-permute-start.6 = (f32[64,2,4,1]{3,0,2,1:T(8,128)S(1)}, f32[64,2,4,1]{3,0,2,1:T(8,128)S(1)}, u32[]{:S(2)}, u32[]{:S(2)}) collective-permute-start(f32[64,2,4,1]{3,0,2,1:T(8,128)S(1)} %get-tuple-element.46), channel_id=1, source_target_pairs={{0,1},{1,2},{2,3},{4,5},{5,6},{6,7},{8,9},{9,10},{10,11},{12,13},{... | collective-permute-start | bytes 6152 | tf_op jit(solution)/shard_map/ppermute | solution.py:13
  44.6 9.3 %collective-permute-start.7 = (f32[64,2,4,1]{3,0,2,1:T(8,128)S(1)}, f32[64,2,4,1]{3,0,2,1:T(8,128)S(1)}, u32[]{:S(2)}, u32[]{:S(2)}) collective-permute-start(f32[64,2,4,1]{3,0,2,1:T(8,128)S(1)} %get-tuple-element.47), channel_id=1, source_target_pairs={{1,0},{2,1},{3,2},{5,4},{6,5},{7,6},{9,8},{10,9},{11,10},{13,12},{... | collective-permute-start | bytes 6152 | tf_op jit(solution)/shard_map/ppermute | solution.py:16
  59.0 12.4 %collective-permute-start.8 = (f32[64,2,2,128]{3,0,2,1:T(8,128)S(1)}, f32[64,2,2,128]{3,0,2,1:T(8,128)S(1)}, u32[]{:S(2)}, u32[]{:S(2)}) collective-permute-start(f32[64,2,2,128]{3,0,2,1:T(8,128)S(1)} %bitcast_multiply_fusion.12), channel_id=1, source_target_pairs={{0,128},{1,129},{2,130},{3,131},{4,132},{5,133},{6,134},{7,135},{8... | collective-permute-start | bytes 393224 | tf_op jit(solution)/shard_map/ppermute | solution.py:24
  74.0 6.0 collective-permute-start.10
  80.2 9.0 %collective-permute-start.11 = (f32[64,2,4,1]{3,0,2,1:T(8,128)S(1)}, f32[64,2,4,1]{3,0,2,1:T(8,128)S(1)}, u32[]{:S(2)}, u32[]{:S(2)}) collective-permute-start(f32[64,2,4,1]{3,0,2,1:T(8,128)S(1)} %get-tuple-element.42), channel_id=1, source_target_pairs={{0,1},{1,2},{2,3},{4,5},{5,6},{6,7},{8,9},{9,10},{10,11},{12,13},{... | collective-permute-start | bytes 6152 | tf_op jit(solution)/shard_map/ppermute | solution.py:13
  82.2 9.0 %collective-permute-start.12 = (f32[64,2,4,1]{3,0,2,1:T(8,128)S(1)}, f32[64,2,4,1]{3,0,2,1:T(8,128)S(1)}, u32[]{:S(2)}, u32[]{:S(2)}) collective-permute-start(f32[64,2,4,1]{3,0,2,1:T(8,128)S(1)} %get-tuple-element.43), channel_id=1, source_target_pairs={{1,0},{2,1},{3,2},{5,4},{6,5},{7,6},{9,8},{10,9},{11,10},{13,12},{... | collective-permute-start | bytes 6152 | tf_op jit(solution)/shard_map/ppermute | solution.py:16
  96.2 5.1 collective-permute-start.13
  100.0 5.3 collective-permute-start.14
  105.5 9.0 %collective-permute-start.15 = (f32[64,2,4,1]{3,0,2,1:T(8,128)S(1)}, f32[64,2,4,1]{3,0,2,1:T(8,128)S(1)}, u32[]{:S(2)}, u32[]{:S(2)}) collective-permute-start(f32[64,2,4,1]{3,0,2,1:T(8,128)S(1)} %get-tuple-element.40), channel_id=1, source_target_pairs={{0,1},{1,2},{2,3},{4,5},{5,6},{6,7},{8,9},{9,10},{10,11},{12,13},{... | collective-permute-start | bytes 6152 | tf_op jit(solution)/shard_map/ppermute | solution.py:13
  107.7 9.3 %collective-permute-start.16 = (f32[64,2,4,1]{3,0,2,1:T(8,128)S(1)}, f32[64,2,4,1]{3,0,2,1:T(8,128)S(1)}, u32[]{:S(2)}, u32[]{:S(2)}) collective-permute-start(f32[64,2,4,1]{3,0,2,1:T(8,128)S(1)} %get-tuple-element.41), channel_id=1, source_target_pairs={{1,0},{2,1},{3,2},{5,4},{6,5},{7,6},{9,8},{10,9},{11,10},{13,12},{... | collective-permute-start | bytes 6152 | tf_op jit(solution)/shard_map/ppermute | solution.py:16
  122.2 11.4 %collective-permute-start.17 = (f32[64,2,2,128]{3,0,2,1:T(8,128)S(1)}, f32[64,2,2,128]{3,0,2,1:T(8,128)S(1)}, u32[]{:S(2)}, u32[]{:S(2)}) collective-permute-start(f32[64,2,2,128]{3,0,2,1:T(8,128)S(1)} %get-tuple-element.21), channel_id=1, source_target_pairs={{0,128},{1,129},{2,130},{3,131},{4,132},{5,133},{6,134},{7,135},{8... | collective-permute-start | bytes 393224 | tf_op jit(solution)/shard_map/ppermute | solution.py:24
  136.3 4.5 collective-permute-start.19
  141.0 9.0 %collective-permute-start.20 = (f32[64,2,4,1]{3,0,2,1:T(8,128)S(1)}, f32[64,2,4,1]{3,0,2,1:T(8,128)S(1)}, u32[]{:S(2)}, u32[]{:S(2)}) collective-permute-start(f32[64,2,4,1]{3,0,2,1:T(8,128)S(1)} %get-tuple-element.38), channel_id=1, source_target_pairs={{0,1},{1,2},{2,3},{4,5},{5,6},{6,7},{8,9},{9,10},{10,11},{12,13},{... | collective-permute-start | bytes 6152 | tf_op jit(solution)/shard_map/ppermute | solution.py:13
  143.2 9.3 %collective-permute-start.21 = (f32[64,2,4,1]{3,0,2,1:T(8,128)S(1)}, f32[64,2,4,1]{3,0,2,1:T(8,128)S(1)}, u32[]{:S(2)}, u32[]{:S(2)}) collective-permute-start(f32[64,2,4,1]{3,0,2,1:T(8,128)S(1)} %get-tuple-element.39), channel_id=1, source_target_pairs={{1,0},{2,1},{3,2},{5,4},{6,5},{7,6},{9,8},{10,9},{11,10},{13,12},{... | collective-permute-start | bytes 6152 | tf_op jit(solution)/shard_map/ppermute | solution.py:16
  157.6 4.8 collective-permute-start.22
  161.0 5.4 collective-permute-start.23
  166.6 9.0 %collective-permute-start.24 = (f32[64,2,4,1]{3,0,2,1:T(8,128)S(1)}, f32[64,2,4,1]{3,0,2,1:T(8,128)S(1)}, u32[]{:S(2)}, u32[]{:S(2)}) collective-permute-start(f32[64,2,4,1]{3,0,2,1:T(8,128)S(1)} %get-tuple-element.36), channel_id=1, source_target_pairs={{0,1},{1,2},{2,3},{4,5},{5,6},{6,7},{8,9},{9,10},{10,11},{12,13},{... | collective-permute-start | bytes 6152 | tf_op jit(solution)/shard_map/ppermute | solution.py:13
  168.5 9.0 %collective-permute-start.25 = (f32[64,2,4,1]{3,0,2,1:T(8,128)S(1)}, f32[64,2,4,1]{3,0,2,1:T(8,128)S(1)}, u32[]{:S(2)}, u32[]{:S(2)}) collective-permute-start(f32[64,2,4,1]{3,0,2,1:T(8,128)S(1)} %get-tuple-element.37), channel_id=1, source_target_pairs={{1,0},{2,1},{3,2},{5,4},{6,5},{7,6},{9,8},{10,9},{11,10},{13,12},{... | collective-permute-start | bytes 6152 | tf_op jit(solution)/shard_map/ppermute | solution.py:16
  182.8 5.1 collective-permute-start.26
  186.6 4.6 collective-permute-start.27
  191.3 9.0 %collective-permute-start.28 = (f32[64,2,4,1]{3,0,2,1:T(8,128)S(1)}, f32[64,2,4,1]{3,0,2,1:T(8,128)S(1)}, u32[]{:S(2)}, u32[]{:S(2)}) collective-permute-start(f32[64,2,4,1]{3,0,2,1:T(8,128)S(1)} %get-tuple-element.34), channel_id=1, source_target_pairs={{0,1},{1,2},{2,3},{4,5},{5,6},{6,7},{8,9},{9,10},{10,11},{12,13},{... | collective-permute-start | bytes 6152 | tf_op jit(solution)/shard_map/ppermute | solution.py:13
  193.3 9.0 %collective-permute-start.29 = (f32[64,2,4,1]{3,0,2,1:T(8,128)S(1)}, f32[64,2,4,1]{3,0,2,1:T(8,128)S(1)}, u32[]{:S(2)}, u32[]{:S(2)}) collective-permute-start(f32[64,2,4,1]{3,0,2,1:T(8,128)S(1)} %get-tuple-element.35), channel_id=1, source_target_pairs={{1,0},{2,1},{3,2},{5,4},{6,5},{7,6},{9,8},{10,9},{11,10},{13,12},{... | collective-permute-start | bytes 6152 | tf_op jit(solution)/shard_map/ppermute | solution.py:16
  207.2 5.1 collective-permute-start.30
  210.9 5.1 collective-permute-start.31
  216.2 9.0 %collective-permute-start.32 = (f32[64,2,4,1]{3,0,2,1:T(8,128)S(1)}, f32[64,2,4,1]{3,0,2,1:T(8,128)S(1)}, u32[]{:S(2)}, u32[]{:S(2)}) collective-permute-start(f32[64,2,4,1]{3,0,2,1:T(8,128)S(1)} %get-tuple-element.32), channel_id=1, source_target_pairs={{0,1},{1,2},{2,3},{4,5},{5,6},{6,7},{8,9},{9,10},{10,11},{12,13},{... | collective-permute-start | bytes 6152 | tf_op jit(solution)/shard_map/ppermute | solution.py:13
  218.2 9.1 %collective-permute-start.33 = (f32[64,2,4,1]{3,0,2,1:T(8,128)S(1)}, f32[64,2,4,1]{3,0,2,1:T(8,128)S(1)}, u32[]{:S(2)}, u32[]{:S(2)}) collective-permute-start(f32[64,2,4,1]{3,0,2,1:T(8,128)S(1)} %get-tuple-element.33), channel_id=1, source_target_pairs={{1,0},{2,1},{3,2},{5,4},{6,5},{7,6},{9,8},{10,9},{11,10},{13,12},{... | collective-permute-start | bytes 6152 | tf_op jit(solution)/shard_map/ppermute | solution.py:16
  231.9 11.5 %collective-permute-start.34 = (f32[64,2,2,128]{3,0,2,1:T(8,128)S(1)}, f32[64,2,2,128]{3,0,2,1:T(8,128)S(1)}, u32[]{:S(2)}, u32[]{:S(2)}) collective-permute-start(f32[64,2,2,128]{3,0,2,1:T(8,128)S(1)} %bitcast.1716), channel_id=1, source_target_pairs={{128,0},{129,1},{130,2},{131,3},{132,4},{133,5},{134,6},{135,7},{1... | collective-permute-start | bytes 393224 | tf_op jit(solution)/shard_map/ppermute | solution.py:24
  246.3 5.9 collective-permute-start.36
  252.4 9.0 %collective-permute-start.37 = (f32[64,2,4,1]{3,0,2,1:T(8,128)S(1)}, f32[64,2,4,1]{3,0,2,1:T(8,128)S(1)}, u32[]{:S(2)}, u32[]{:S(2)}) collective-permute-start(f32[64,2,4,1]{3,0,2,1:T(8,128)S(1)} %get-tuple-element.28), channel_id=1, source_target_pairs={{0,1},{1,2},{2,3},{4,5},{5,6},{6,7},{8,9},{9,10},{10,11},{12,13},{... | collective-permute-start | bytes 6152 | tf_op jit(solution)/shard_map/ppermute | solution.py:13
  254.8 9.3 %collective-permute-start.38 = (f32[64,2,4,1]{3,0,2,1:T(8,128)S(1)}, f32[64,2,4,1]{3,0,2,1:T(8,128)S(1)}, u32[]{:S(2)}, u32[]{:S(2)}) collective-permute-start(f32[64,2,4,1]{3,0,2,1:T(8,128)S(1)} %get-tuple-element.29), channel_id=1, source_target_pairs={{1,0},{2,1},{3,2},{5,4},{6,5},{7,6},{9,8},{10,9},{11,10},{13,12},{... | collective-permute-start | bytes 6152 | tf_op jit(solution)/shard_map/ppermute | solution.py:16
  269.0 5.7 collective-permute-start.39
  276.3 9.0 %collective-permute-start.41 = (f32[64,2,4,1]{3,0,2,1:T(8,128)S(1)}, f32[64,2,4,1]{3,0,2,1:T(8,128)S(1)}, u32[]{:S(2)}, u32[]{:S(2)}) collective-permute-start(f32[64,2,4,1]{3,0,2,1:T(8,128)S(1)} %get-tuple-element.26), channel_id=1, source_target_pairs={{0,1},{1,2},{2,3},{4,5},{5,6},{6,7},{8,9},{9,10},{10,11},{12,13},{... | collective-permute-start | bytes 6152 | tf_op jit(solution)/shard_map/ppermute | solution.py:13
  278.4 9.3 %collective-permute-start.42 = (f32[64,2,4,1]{3,0,2,1:T(8,128)S(1)}, f32[64,2,4,1]{3,0,2,1:T(8,128)S(1)}, u32[]{:S(2)}, u32[]{:S(2)}) collective-permute-start(f32[64,2,4,1]{3,0,2,1:T(8,128)S(1)} %get-tuple-element.27), channel_id=1, source_target_pairs={{1,0},{2,1},{3,2},{5,4},{6,5},{7,6},{9,8},{10,9},{11,10},{13,12},{... | collective-permute-start | bytes 6152 | tf_op jit(solution)/shard_map/ppermute | solution.py:16
  292.3 11.6 %collective-permute-start.43 = (f32[64,2,2,128]{3,0,2,1:T(8,128)S(1)}, f32[64,2,2,128]{3,0,2,1:T(8,128)S(1)}, u32[]{:S(2)}, u32[]{:S(2)}) collective-permute-start(f32[64,2,2,128]{3,0,2,1:T(8,128)S(1)} %bitcast.1715), channel_id=1, source_target_pairs={{128,0},{129,1},{130,2},{131,3},{132,4},{133,5},{134,6},{135,7},{1... | collective-permute-start | bytes 393224 | tf_op jit(solution)/shard_map/ppermute | solution.py:24
  307.1 6.7 collective-permute-start.44
  309.5 5.2 collective-permute-start.45
  314.8 9.0 %collective-permute-start.46 = (f32[64,2,4,1]{3,0,2,1:T(8,128)S(1)}, f32[64,2,4,1]{3,0,2,1:T(8,128)S(1)}, u32[]{:S(2)}, u32[]{:S(2)}) collective-permute-start(f32[64,2,4,1]{3,0,2,1:T(8,128)S(1)} %get-tuple-element.24), channel_id=1, source_target_pairs={{0,1},{1,2},{2,3},{4,5},{5,6},{6,7},{8,9},{9,10},{10,11},{12,13},{... | collective-permute-start | bytes 6152 | tf_op jit(solution)/shard_map/ppermute | solution.py:13
  316.8 9.0 %collective-permute-start.47 = (f32[64,2,4,1]{3,0,2,1:T(8,128)S(1)}, f32[64,2,4,1]{3,0,2,1:T(8,128)S(1)}, u32[]{:S(2)}, u32[]{:S(2)}) collective-permute-start(f32[64,2,4,1]{3,0,2,1:T(8,128)S(1)} %get-tuple-element.25), channel_id=1, source_target_pairs={{1,0},{2,1},{3,2},{5,4},{6,5},{7,6},{9,8},{10,9},{11,10},{13,12},{... | collective-permute-start | bytes 6152 | tf_op jit(solution)/shard_map/ppermute | solution.py:16
  335.1 396.1 %all-reduce.17.cloned.1.call-start = ((), (), s32[]{:S(2)}) async-start(), calls=%async_computation.1 | async-start | bytes 3538944 | tf_op jit(solution)/shard_map/psum | solution.py:147
  335.2 5.1 collective-permute-start.48
  339.0 4.9 collective-permute-start.49
  344.0 91.1 %collective-permute-start.50 = (f32[64,2,4,1]{3,0,2,1:T(8,128)S(1)}, f32[64,2,4,1]{3,0,2,1:T(8,128)S(1)}, u32[]{:S(2)}, u32[]{:S(2)}) collective-permute-start(f32[64,2,4,1]{3,0,2,1:T(8,128)S(1)} %get-tuple-element.22), channel_id=1, source_target_pairs={{0,1},{1,2},{2,3},{4,5},{5,6},{6,7},{8,9},{9,10},{10,11},{12,13},{... | collective-permute-start | bytes 6152 | tf_op jit(solution)/shard_map/ppermute | solution.py:13
  345.9 89.2 %collective-permute-start.51 = (f32[64,2,4,1]{3,0,2,1:T(8,128)S(1)}, f32[64,2,4,1]{3,0,2,1:T(8,128)}, u32[]{:S(2)}, u32[]{:S(2)}) collective-permute-start(f32[64,2,4,1]{3,0,2,1:T(8,128)S(1)} %get-tuple-element.23), channel_id=1, source_target_pairs={{1,0},{2,1},{3,2},{5,4},{6,5},{7,6},{9,8},{10,9},{11,10},{13,12},{... | collective-permute-start | bytes 6152 | tf_op jit(solution)/shard_map/ppermute | solution.py:16
  (10 other events, 53.6 us)
Sparse Core Ops, SparseCore 0:
  335.3 65.7 all-reduce.14
  458.2 272.9 all-reduce.16
